TPU v7x, 32 devices: a whole 2x2x4 slice. The times are simulated.
32 devices in a mesh: group: 4 (over x, core), mp: 8 (over z, y).
Axes of the slice: x: 2, y: 2, z: 4, core: 2. Of those that a mesh axis runs over, the one named last changes fastest.
Arguments:
- tokens: bfloat16 [4096, 8192], P(('group', 'mp')), may hold values from -36 to 36
- cached_update: bfloat16 [4096, 8192], P('group', 'mp'), may hold values from -3 to 3
- norm_gain: float32 [8192], replicated, may hold values from 0.25 to 1.75
- gate_weight: bfloat16 [8192, 14336], P('group', 'mp'), may hold values from -0.0625 to 0.0625
- up_weight: bfloat16 [8192, 14336], P('group', 'mp'), may hold values from -0.0625 to 0.0625
- down_weight: bfloat16 [14336, 8192], P('mp', 'group'), may hold values from -0.0625 to 0.0625
- stale_blocks: int32 [4, 2], P('group'), may hold values from -1 to 7, as said below
- stale_count: int32 [4], replicated, may hold values from 0 to 2, as said below
- lengths: int32 [4], P('group'), may hold values from 512 to 1024, as said below
Outputs:
- refreshed: bfloat16 [4096, 8192], P('group', 'mp')
Inputs may be any that keep to these rules, and one draw needn't show every extreme that they name: `stale_count`: the counts sum to exactly 4. At least a quarter of the groups have 2, at least a quarter have none. A group's count never exceeds the number of its blocks that begin below its length. `stale_blocks`: row g holds stale_count[g] distinct block numbers, each of a block that begins below lengths[g], in any order, then -1 in the other places. Some group lists block 7. `lengths`: some request has 1024 tokens.
All inputs are finite; a program needn't handle non-finite values.
Results may differ from a plain program's by a relative error of at most 0.0035.
Values may be sent and summed in bfloat16 or wider, within the bound.
A program may use at most 256 MiB of HBM per device.

v0:
```python
import jax
import jax.numpy as jnp
from jax import lax
from jax.sharding import PartitionSpec as P

BLK = 128
epsilon = 1e-05


def normalize(row_data, norm_gain):
    values = row_data.astype(jnp.float32)
    mean_sq = jnp.mean(values * values, axis=-1, keepdims=True)
    return (values * lax.rsqrt(mean_sq + epsilon) * norm_gain).astype(jnp.bfloat16)


def refresh(slots, norm_gain, gate_weight, up_weight, down_weight):
    slot_count = slots.shape[0]
    full_rows = lax.all_gather(slots, "mp", axis=2, tiled=True)
    row_data = full_rows.reshape(slot_count * BLK, full_rows.shape[2])
    normed = normalize(row_data, norm_gain)
    gate_vals = jnp.dot(
        normed,
        lax.all_gather(gate_weight, "group", axis=0, tiled=True),
        preferred_element_type=jnp.float32,
    )
    up_vals = jnp.dot(
        normed,
        lax.all_gather(up_weight, "group", axis=0, tiled=True),
        preferred_element_type=jnp.float32,
    )
    hidden = (jax.nn.silu(gate_vals) * up_vals).astype(jnp.bfloat16)
    partial_value = jnp.dot(
        hidden,
        lax.all_gather(down_weight, "group", axis=1, tiled=True),
        preferred_element_type=jnp.float32,
    )
    update = lax.psum_scatter(
        partial_value.astype(jnp.bfloat16), "mp", scatter_dimension=1, tiled=True
    ).astype(jnp.float32)
    return update.reshape(slot_count, BLK, update.shape[1])


def body(
    tokens,
    cached_update,
    norm_gain,
    gate_weight,
    up_weight,
    down_weight,
    stale_blocks,
    stale_count,
    lengths,
):
    n_group = lax.axis_size("group")
    columns = lax.all_to_all(tokens, "mp", split_axis=1, concat_axis=0, tiled=True)
    seq_rows, col_width = columns.shape
    block_total = seq_rows // BLK
    column_blocks = columns.reshape(block_total, BLK, col_width)
    group_id = lax.axis_index("group")
    group_ids = jnp.arange(n_group, dtype=jnp.int32)
    own_mask = group_ids == group_id
    own_count = jnp.sum(jnp.where(own_mask, stale_count, 0))
    own_list = stale_blocks[0]
    list_size = stale_blocks.shape[1]
    block_ids = jnp.arange(block_total, dtype=jnp.int32)
    picker = (own_list[:, None] == block_ids[None, :]).astype(jnp.bfloat16)
    own_rows = jnp.einsum(
        "pb,brc->prc", picker, column_blocks, preferred_element_type=jnp.float32
    ).astype(jnp.bfloat16)
    results = refresh(own_rows, norm_gain, gate_weight, up_weight, down_weight)
    positions = jnp.arange(list_size, dtype=jnp.int32)
    listed = (own_list[None, :] == block_ids[:, None]) & (positions[None, :] < own_count)
    block_update = jnp.einsum(
        "bp,prc->brc", listed.astype(jnp.float32), results, precision=lax.Precision.HIGHEST
    )
    stale_rows = jnp.any(listed, axis=1)[:, None, None]
    row_pos = block_ids[:, None] * BLK + jnp.arange(BLK, dtype=jnp.int32)[None, :]
    live_rows = (row_pos < lengths[0])[:, :, None]
    cache_blocks = cached_update.reshape(block_total, BLK, col_width).astype(jnp.float32)
    combined = column_blocks.astype(jnp.float32) + jnp.where(stale_rows, block_update, cache_blocks)
    refreshed = jnp.where(live_rows, combined, jnp.float32(0.0))
    return refreshed.astype(jnp.bfloat16).reshape(seq_rows, col_width)


def solution(mesh):
    in_specs = (
        P(("group", "mp"), None),
        P("group", "mp"),
        P(),
        P("group", "mp"),
        P("group", "mp"),
        P("mp", "group"),
        P("group", None),
        P(),
        P("group"),
    )
    out_specs = P("group", "mp")
    return jax.shard_map(body, mesh=mesh, in_specs=in_specs, out_specs=out_specs, check_vma=False)
```

profile of v0, /device:TPU:0, one launch (start us, length us, event | category | flops | bytes accessed | tf_op | source)
XLA Modules:
  0.0 816.9 jit_solution(3097391666787981656)
XLA Ops:
  6.5 0.0 all-gather.5.cloned.1.call-start
  6.5 4.1 copy.28
  10.6 0.0 copy-start.4
  10.6 2.9 copy.29
  13.5 55.3 %all_to_all.16 = bf16[128,8,1024]{2,0,1:T(8,128)(2,1)S(1)} all-to-all(bf16[128,8,1024]{2,0,1:T(8,128)(2,1)S(1)} %copy.29), channel_id=1, replica_groups=mesh['group'=4,'mp'=8] {'mp'}, dimensions={1} | all-to-all | bytes 4194304 | tf_op jit(solution)/shard_map/all_to_all | solution.py:55
  68.8 0.0 copy-start.1
  68.8 1.3 copy-done.1
  70.1 0.0 copy-done.4
  70.1 1.4 fusion.6
  71.6 0.9 copy.53
  72.5 0.0 all-gather.5.cloned.1.call-update
  72.6 0.0 all-gather.7.cloned.1.call-start
  72.6 0.7 all-gather.7.cloned.1.call-update
  73.3 0.0 all-gather.11.cloned.1.call-start
  73.3 0.7 all-gather.11.cloned.1.call-update
  74.0 0.0 copy-start.3
  74.0 0.0 all-gather.9.cloned.1.call-start
  74.1 0.5 all-gather.9.cloned.1.call-update
  74.6 0.2 reduce-scatter.2.cloned.1.call-start
  74.9 69.6 %all-gather.5.cloned.1.call-done = bf16[2,128,8192]{2,1,0:T(8,128)(2,1)} async-done(((bf16[2,128,1024]{2,1,0:T(8,128)(2,1)}), bf16[2,128,8192]{2,1,0:T(8,128)(2,1)}) %all-gather.5.cloned.1.call-update) | async-done | bytes 4194320 | tf_op jit(solution)/shard_map/all_gather | solution.py:18
  144.5 0.0 copy-start
  144.5 3.3 multiply_reduce_fusion
  147.8 0.0 copy-done.3
  147.8 0.2 copy-done
  147.9 3.4 fusion.1
  151.3 171.3 %all-gather.7.cloned.1.call-done = bf16[8192,1792]{1,0:T(8,128)(2,1)} async-done(((bf16[2048,1792]{1,0:T(8,128)(2,1)}), bf16[8192,1792]{1,0:T(8,128)(2,1)}) %all-gather.7.cloned.1.call-update) | async-done | bytes 29360144 | tf_op jit(solution)/shard_map/all_gather | solution.py:23
  322.6 17.9 %fusion.26 = f32[256,1792]{1,0:T(8,128)S(1)} fusion(bf16[256,8192]{1,0:T(8,128)(2,1)} %fusion.1, bf16[8192,1792]{1,0:T(8,128)(2,1)} %all-gather.7.cloned.1.call-done), kind=kOutput, calls=%fused_computation.38 | convolution fusion | flops 7516192768 | bytes 35389440 | tf_op jit(solution)/shard_map/dot_general | solution.py:21
  340.5 161.7 %all-gather.11.cloned.1.call-done = bf16[1792,8192]{1,0:T(8,128)(2,1)} async-done(((bf16[1792,2048]{1,0:T(8,128)(2,1)}), bf16[1792,8192]{1,0:T(8,128)(2,1)}) %all-gather.11.cloned.1.call-update) | async-done | bytes 29360144 | tf_op jit(solution)/shard_map/all_gather | solution.py:34
  502.2 179.4 %all-gather.9.cloned.1.call-done = bf16[8192,1792]{1,0:T(8,128)(2,1)} async-done(((bf16[2048,1792]{1,0:T(8,128)(2,1)}), bf16[8192,1792]{1,0:T(8,128)(2,1)}) %all-gather.9.cloned.1.call-update) | async-done | bytes 29360144 | tf_op jit(solution)/shard_map/all_gather | solution.py:28
  681.6 29.4 %convolution_convert_fusion = bf16[256,8192]{1,0:T(8,128)(2,1)} fusion(bf16[1792,8192]{1,0:T(8,128)(2,1)} %all-gather.11.cloned.1.call-done, bf16[256,8192]{1,0:T(8,128)(2,1)} %fusion.1, bf16[8192,1792]{1,0:T(8,128)(2,1)} %all-gather.9.cloned.1.call-done, f32[256,1792]{1,0:T(8,128)S(1)} %fusion.26), kind=kOutput, calls=%fused_computation | convolution fusion | flops 15037235200 | bytes 68943872 | tf_op jit(solution)/shard_map/dot_general | solution.py:32
  711.0 0.0 reduce-scatter.2.cloned.1.call-update
  711.0 0.0 copy-start.6
  711.0 0.0 copy-start.5
  711.1 0.0 copy-start.2
  711.1 4.2 convert.2
  715.9 0.0 copy-done.6
  715.9 0.6 fusion.22
  716.5 0.5 iota_compare_fusion
  717.1 0.0 copy-done.5
  717.1 0.1 fusion.20
  717.2 82.7 %reduce-scatter.2.cloned.1.call-done = bf16[256,1024]{1,0:T(8,128)(2,1)} async-done(((bf16[256,8192]{1,0:T(8,128)(2,1)}), bf16[256,1024]{1,0:T(8,128)(2,1)}) %reduce-scatter.2.cloned.1.call-update) | async-done | bytes 524304 | tf_op jit(solution)/shard_map/reduce_scatter | solution.py:37
  799.9 0.0 copy-done.2
  799.9 8.0 fusion.4
  807.9 2.5 copy.36
  (3 shorter events, 0.0 us)
Async XLA Ops:
  6.5 138.0 %all-gather.5.cloned.1.call-start = ((), (), s32[]{:S(2)}) async-start(), calls=%async_computation.2 | async-start | bytes 4718592 | tf_op jit(solution)/shard_map/all_gather | solution.py:18
  10.6 59.5 %copy-start.4 = (s32[1,2]{1,0:T(1,128)S(1)}, s32[1,2]{1,0:T(1,128)}, u32[]{:S(2)}) copy-start(s32[1,2]{1,0:T(1,128)} %param.15) | copy-start | bytes 28
  68.8 1.3 copy-start.1
  72.6 250.1 %all-gather.7.cloned.1.call-start = ((), (), s32[]{:S(2)}) async-start(), calls=%async_computation.3 | async-start | bytes 36700160 | tf_op jit(solution)/shard_map/all_gather | solution.py:23
  73.3 428.9 %all-gather.11.cloned.1.call-start = ((), (), s32[]{:S(2)}) async-start(), calls=%async_computation.5 | async-start | bytes 36700160 | tf_op jit(solution)/shard_map/all_gather | solution.py:34
  74.0 73.7 %copy-start.3 = (f32[8192]{0:T(1024)S(1)}, f32[8192]{0:T(1024)}, u32[]{:S(2)}) copy-start(f32[8192]{0:T(1024)} %param.11) | copy-start | bytes 98308
  74.0 607.6 %all-gather.9.cloned.1.call-start = ((), (), s32[]{:S(2)}) async-start(), calls=%async_computation.4 | async-start | bytes 36700160 | tf_op jit(solution)/shard_map/all_gather | solution.py:28
  74.6 725.3 %reduce-scatter.2.cloned.1.call-start = ((), (), s32[]{:S(2)}) async-start(), calls=%async_computation.6 | async-start | bytes 4718592 | tf_op jit(solution)/shard_map/reduce_scatter | solution.py:37
  144.5 3.4 copy-start
  711.0 4.9 copy-start.6
  711.0 6.0 copy-start.5
  711.1 88.8 %copy-start.2 = (bf16[128,8,1024]{2,0,1:T(8,128)(2,1)S(1)}, bf16[128,8,1024]{2,0,1:T(8,128)(2,1)}, u32[]{:S(2)}) copy-start(bf16[128,8,1024]{2,0,1:T(8,128)(2,1)} %copy-done.1) | copy-start | bytes 6291460
Sparse Core Ops, SparseCore 0:
  72.7 71.7 all-gather.4
  146.1 176.5 all-gather.6
  324.2 177.9 all-gather.10
  503.6 177.9 all-gather.8
  711.2 88.6 reduce-scatter.1
where the time goes:
time: 817 us
  waiting for transfers between devices  667 us (82%)
  matrix products  56.7 us (7%)
  blocking collectives  55.3 us (7%)
  between operations  13.9 us (2%)
  other arithmetic  12.1 us (1%)
  local copies, waits for them, and re-layouts  11.9 us (1%)
    all_gather x1, waiting for transfers between devices, refresh(): lax.all_gather(up_weight, 'group', axis=0, tiled=True)  179 us
    all_gather x1, waiting for transfers between devices, refresh(): lax.all_gather(gate_weight, 'group', axis=0, tiled=True)  171 us
    all_gather x1, waiting for transfers between devices, refresh(): lax.all_gather(down_weight, 'group', axis=1, tiled=True)  162 us
    reduce_scatter x1, waiting for transfers between devices, refresh(): lax.psum_scatter(partial_value.astype(jnp.bfloat16), 'mp', scatter_dimens...  82.7 us
    all_gather x1, waiting for transfers between devices, refresh(): full_rows = lax.all_gather(slots, 'mp', axis=2, tiled=True)  69.6 us
    all_to_all x1, blocking collectives, body(): lax.all_to_all(tokens, 'mp', split_axis=1, concat_axis=0, tiled=True)  55.3 us
    dot_general x1, matrix products, refresh(): jnp.dot(hidden, lax.all_gather(down_weight, 'group', axis=1, tiled=True),...  29.4 us
    dot_general x1, matrix products, refresh(): jnp.dot(normed, lax.all_gather(gate_weight, 'group', axis=0, tiled=True),...  17.9 us
  transfers between devices with their start and end apart: 5, of which 5 were waited for; matrix products, arithmetic and copies ran while one was open for 4% of the time, Pallas kernels for 0%

commit v1 on v0

--- a/solution.py
+++ b/solution.py
@@ -52,7 +52,10 @@
     lengths,
 ):
     n_group = lax.axis_size("group")
-    columns = lax.all_to_all(tokens, "mp", split_axis=1, concat_axis=0, tiled=True)
+    columns = jnp.concatenate(
+        lax.all_to_all(jnp.stack(jnp.split(tokens, lax.axis_size("mp"), axis=1)), "mp", 0, 0),
+        axis=0,
+    )
     seq_rows, col_width = columns.shape
     block_total = seq_rows // BLK
     column_blocks = columns.reshape(block_total, BLK, col_width)

time: 817 us -> 814 us (level)
  no operation moved by 1% of the time
where the time goes in v1:
time: 814 us
  waiting for transfers between devices  666 us (82%)
  matrix products  56.8 us (7%)
  blocking collectives  55.3 us (7%)
  between operations  14 us (2%)
  other arithmetic  12.3 us (2%)
  local copies, waits for them, and re-layouts  9.05 us (1%)
    all_gather x1, waiting for transfers between devices, refresh(): lax.all_gather(up_weight, 'group', axis=0, tiled=True)  179 us
    all_gather x1, waiting for transfers between devices, refresh(): lax.all_gather(gate_weight, 'group', axis=0, tiled=True)  171 us
    all_gather x1, waiting for transfers between devices, refresh(): lax.all_gather(down_weight, 'group', axis=1, tiled=True)  162 us
    reduce_scatter x1, waiting for transfers between devices, refresh(): lax.psum_scatter(partial_value.astype(jnp.bfloat16), 'mp', scatter_dimens...  82.4 us
    all_gather x1, waiting for transfers between devices, refresh(): full_rows = lax.all_gather(slots, 'mp', axis=2, tiled=True)  69.6 us
    all_to_all x1, blocking collectives, body(): lax.all_to_all(jnp.stack(jnp.split(tokens, lax.axis_size('mp'), axis=1)),...  55.3 us
    dot_general x1, matrix products, refresh(): jnp.dot(hidden, lax.all_gather(down_weight, 'group', axis=1, tiled=True),...  29.4 us
    dot_general x1, matrix products, refresh(): jnp.dot(normed, lax.all_gather(gate_weight, 'group', axis=0, tiled=True),...  18 us
  transfers between devices with their start and end apart: 5, of which 5 were waited for; matrix products, arithmetic and copies ran while one was open for 4% of the time, Pallas kernels for 0%

profile of v1, /device:TPU:0, one launch (start us, length us, event | category | flops | bytes accessed | tf_op | source)
XLA Modules:
  0.0 814.1 jit_solution(5898609872480830965)
XLA Ops:
  6.5 0.0 copy-start.3
  6.5 0.0 all-gather.5.cloned.1.call-start
  6.5 1.1 bitcast_dynamic-update-slice_fusion.7
  7.7 1.0 bitcast_dynamic-update-slice_fusion.6
  8.6 1.0 bitcast_dynamic-update-slice_fusion.5
  9.6 1.0 bitcast_dynamic-update-slice_fusion.4
  10.6 0.0 copy-done.3
  10.7 0.0 copy-start.5
  10.7 55.3 %all_to_all.5 = bf16[8,128,1024]{2,1,0:T(8,128)(2,1)S(1)} all-to-all(bf16[8,128,1024]{2,1,0:T(8,128)(2,1)S(1)} %bitcast_dynamic-update-slice_fusion), channel_id=1, replica_groups=mesh['group'=4,'mp'=8] {'mp'}, dimensions={0} | all-to-all | bytes 4194304 | tf_op jit(solution)/shard_map/all_to_all | solution.py:56
  66.1 0.0 copy-start.1
  66.1 1.3 copy-done.1
  67.4 0.0 copy-done.5
  67.4 1.4 fusion.6
  68.8 0.9 copy.58
  69.8 0.0 all-gather.5.cloned.1.call-update
  69.8 0.0 all-gather.7.cloned.1.call-start
  69.8 0.7 all-gather.7.cloned.1.call-update
  70.5 0.0 all-gather.11.cloned.1.call-start
  70.6 0.7 all-gather.11.cloned.1.call-update
  71.3 0.0 all-gather.9.cloned.1.call-start
  71.3 0.0 copy-start.4
  71.3 0.5 all-gather.9.cloned.1.call-update
  71.9 0.2 reduce-scatter.2.cloned.1.call-start
  72.1 69.6 %all-gather.5.cloned.1.call-done = bf16[2,128,8192]{2,1,0:T(8,128)(2,1)} async-done(((bf16[2,128,1024]{2,1,0:T(8,128)(2,1)}), bf16[2,128,8192]{2,1,0:T(8,128)(2,1)}) %all-gather.5.cloned.1.call-update) | async-done | bytes 4194320 | tf_op jit(solution)/shard_map/all_gather | solution.py:18
  141.7 0.0 copy-start
  141.7 3.3 multiply_reduce_fusion
  145.0 0.0 copy-done.4
  145.0 0.2 copy-done
  145.2 3.4 fusion.1
  148.6 171.3 %all-gather.7.cloned.1.call-done = bf16[8192,1792]{1,0:T(8,128)(2,1)} async-done(((bf16[2048,1792]{1,0:T(8,128)(2,1)}), bf16[8192,1792]{1,0:T(8,128)(2,1)}) %all-gather.7.cloned.1.call-update) | async-done | bytes 29360144 | tf_op jit(solution)/shard_map/all_gather | solution.py:23
  319.9 18.0 %fusion.25 = f32[256,1792]{1,0:T(8,128)S(1)} fusion(bf16[256,8192]{1,0:T(8,128)(2,1)} %fusion.1, bf16[8192,1792]{1,0:T(8,128)(2,1)} %all-gather.7.cloned.1.call-done), kind=kOutput, calls=%fused_computation.45 | convolution fusion | flops 7516192768 | bytes 35389440 | tf_op jit(solution)/shard_map/dot_general | solution.py:21
  337.8 161.6 %all-gather.11.cloned.1.call-done = bf16[1792,8192]{1,0:T(8,128)(2,1)} async-done(((bf16[1792,2048]{1,0:T(8,128)(2,1)}), bf16[1792,8192]{1,0:T(8,128)(2,1)}) %all-gather.11.cloned.1.call-update) | async-done | bytes 29360144 | tf_op jit(solution)/shard_map/all_gather | solution.py:34
  499.4 179.4 %all-gather.9.cloned.1.call-done = bf16[8192,1792]{1,0:T(8,128)(2,1)} async-done(((bf16[2048,1792]{1,0:T(8,128)(2,1)}), bf16[8192,1792]{1,0:T(8,128)(2,1)}) %all-gather.9.cloned.1.call-update) | async-done | bytes 29360144 | tf_op jit(solution)/shard_map/all_gather | solution.py:28
  678.9 29.4 %convolution_convert_fusion = bf16[256,8192]{1,0:T(8,128)(2,1)} fusion(bf16[1792,8192]{1,0:T(8,128)(2,1)} %all-gather.11.cloned.1.call-done, bf16[256,8192]{1,0:T(8,128)(2,1)} %fusion.1, bf16[8192,1792]{1,0:T(8,128)(2,1)} %all-gather.9.cloned.1.call-done, f32[256,1792]{1,0:T(8,128)S(1)} %fusion.25), kind=kOutput, calls=%fused_computation | convolution fusion | flops 15037235200 | bytes 68943872 | tf_op jit(solution)/shard_map/dot_general | solution.py:32
  708.3 0.0 reduce-scatter.2.cloned.1.call-update
  708.3 0.0 copy-start.7
  708.3 0.0 copy-start.6
  708.3 0.0 copy-start.2
  708.3 4.2 convert.2
  713.2 0.0 copy-done.7
  713.2 0.7 fusion.21
  713.9 0.7 iota_compare_fusion
  714.6 0.0 copy-done.6
  714.6 0.1 fusion.19
  714.7 82.4 %reduce-scatter.2.cloned.1.call-done = bf16[256,1024]{1,0:T(8,128)(2,1)} async-done(((bf16[256,8192]{1,0:T(8,128)(2,1)}), bf16[256,1024]{1,0:T(8,128)(2,1)}) %reduce-scatter.2.cloned.1.call-update) | async-done | bytes 524304 | tf_op jit(solution)/shard_map/reduce_scatter | solution.py:37
  797.2 0.0 copy-done.2
  797.2 8.0 fusion.4
  805.1 2.5 copy.43
  (7 shorter events, 0.1 us)
Async XLA Ops:
  6.5 4.0 copy-start.3
  6.5 135.2 %all-gather.5.cloned.1.call-start = ((), (), s32[]{:S(2)}) async-start(), calls=%async_computation.2 | async-start | bytes 4718592 | tf_op jit(solution)/shard_map/all_gather | solution.py:18
  10.7 56.7 %copy-start.5 = (s32[1,2]{1,0:T(1,128)S(1)}, s32[1,2]{1,0:T(1,128)}, u32[]{:S(2)}) copy-start(s32[1,2]{1,0:T(1,128)} %param.15) | copy-start | bytes 28
  66.1 1.3 copy-start.1
  69.8 250.1 %all-gather.7.cloned.1.call-start = ((), (), s32[]{:S(2)}) async-start(), calls=%async_computation.3 | async-start | bytes 36700160 | tf_op jit(solution)/shard_map/all_gather | solution.py:23
  70.5 428.9 %all-gather.11.cloned.1.call-start = ((), (), s32[]{:S(2)}) async-start(), calls=%async_computation.5 | async-start | bytes 36700160 | tf_op jit(solution)/shard_map/all_gather | solution.py:34
  71.3 607.6 %all-gather.9.cloned.1.call-start = ((), (), s32[]{:S(2)}) async-start(), calls=%async_computation.4 | async-start | bytes 36700160 | tf_op jit(solution)/shard_map/all_gather | solution.py:28
  71.3 73.7 %copy-start.4 = (f32[8192]{0:T(1024)S(1)}, f32[8192]{0:T(1024)}, u32[]{:S(2)}) copy-start(f32[8192]{0:T(1024)} %param.11) | copy-start | bytes 98308
  71.9 725.3 %reduce-scatter.2.cloned.1.call-start = ((), (), s32[]{:S(2)}) async-start(), calls=%async_computation.6 | async-start | bytes 4718592 | tf_op jit(solution)/shard_map/reduce_scatter | solution.py:37
  141.7 3.4 copy-start
  708.3 4.9 copy-start.7
  708.3 6.3 copy-start.6
  708.3 88.8 %copy-start.2 = (bf16[8,128,1024]{2,1,0:T(8,128)(2,1)S(1)}, bf16[8,128,1024]{2,1,0:T(8,128)(2,1)}, u32[]{:S(2)}) copy-start(bf16[8,128,1024]{2,1,0:T(8,128)(2,1)} %copy-done.1) | copy-start | bytes 6291460
Sparse Core Ops, SparseCore 0:
  69.9 71.7 all-gather.4
  143.3 176.5 all-gather.6
  321.4 177.9 all-gather.10
  500.9 177.9 all-gather.8
  708.4 88.6 reduce-scatter.1
